TPU v7x, 512 devices: a whole 4x8x8 slice. The times are simulated.
512 devices in a mesh: seq: 128 (over x, y_hi, z, core), tp: 4 (over y_lo).
Axes of the slice: x: 4, y: 8 (y_hi: 2, y_lo: 4; y = y_hi * 4 + y_lo), z: 8, core: 2. Of those that a mesh axis runs over, the one named last changes fastest.
Arguments:
- tokens: bfloat16 [16384, 2560], P('seq', 'tp'), may hold values from -6 to 6
- seg_ids: int32 [16384], P('seq'), may hold values from 0 to 31, never falling along the last dimension, each value on 1 to 4096 neighbouring positions
- norm_gain: bfloat16 [2560], replicated, may hold values from 0.099609375 to 1.8984375
- w_query: bfloat16 [2560, 2048], P('seq', 'tp'), may hold values from -3 to 3
- w_keyval: bfloat16 [2560, 512], P('seq'), may hold values from -1 to 1
- w_out: bfloat16 [2048, 2560], P('tp', 'seq'), may hold values from -0.125 to 0.125
Outputs:
- hidden: bfloat16 [16384, 2560], P('seq', 'tp')
- kv_cache: bfloat16 [16384, 512], P('seq')
Inputs may be any that keep to these rules, and one draw needn't show every extreme that they name: `seg_ids`: ids never fall along the stream; each of the 32 requests holds 1 to 4096 consecutive tokens, one exactly 4096.
All inputs are finite; a program needn't handle non-finite values.
Results may differ from a plain program's by a relative error of at most 0.0085.
Values may be sent and summed in bfloat16 or wider, within the bound.
No kernel may reach another device: no remote copies, remote signals or barrier semaphores. Data moves between devices by JAX's collectives and lax.ppermute only.
A program may use at most 64 MiB of HBM per device.

v0:
```python
import jax
import jax.numpy as jnp
from jax import lax
from jax.sharding import PartitionSpec as P

HD = 256
WINDOW = 2048
SEG_MEAN = 512


def from_behind(x, axis, by):
    devices = lax.axis_size(axis)
    pairs = [(i, i + by) for i in range(devices) if 0 <= i + by < devices]
    return lax.ppermute(x, axis, pairs)


def rms_norm(values, gain):
    wide = values.astype(jnp.float32)
    scaled = wide * lax.rsqrt(jnp.mean(wide * wide, axis=-1, keepdims=True) + 1e-06)
    return (scaled * gain.astype(jnp.float32)).astype(jnp.bfloat16)


def rotate(tensor, positions):
    quarter = tensor.shape[-1] // 4
    freq = 10000.0 ** (-jnp.arange(quarter, dtype=jnp.float32) / quarter)
    angle = positions[:, None, None] * freq
    cosine = jnp.cos(angle)
    sine = jnp.sin(angle)
    first = tensor[..., :quarter]
    second = tensor[..., quarter : 2 * quarter]
    return jnp.concatenate(
        [
            first * cosine - second * sine,
            second * cosine + first * sine,
            tensor[..., 2 * quarter :],
        ],
        axis=-1,
    )


def per_device(tokens, seg_ids, norm_gain, w_query, w_keyval, w_out):
    tok_rows = tokens.shape[0]
    seq_count = lax.axis_size("seq")
    my_index = lax.axis_index("seq")
    gathered = lax.all_gather(tokens, "tp", axis=1, tiled=True)
    normed = rms_norm(gathered, norm_gain)
    seg_total = tok_rows * seq_count // SEG_MEAN
    labels = jnp.arange(seg_total, dtype=jnp.int32)
    below = jnp.sum((seg_ids[None, :] < labels[:, None]).astype(jnp.int32), axis=1)
    starts = lax.psum(below, "seq")
    own_start = jnp.sum(jnp.where(seg_ids[:, None] == labels[None, :], starts[None, :], 0), axis=1)
    token_index = my_index * tok_rows + jnp.arange(tok_rows, dtype=jnp.int32)
    positions = (token_index - own_start).astype(jnp.float32)
    query_raw = jnp.dot(
        normed,
        lax.all_gather(w_query, "seq", axis=0, tiled=True),
        preferred_element_type=jnp.float32,
    )
    keyval_raw = jnp.dot(
        normed,
        lax.all_gather(w_keyval, "seq", axis=0, tiled=True),
        preferred_element_type=jnp.float32,
    )
    local_heads = w_query.shape[1] // HD
    queries = rotate(query_raw.reshape(tok_rows, local_heads, HD), positions).astype(jnp.bfloat16)
    key_rows = rotate(keyval_raw[:, None, :HD], positions)[:, 0, :]
    kv_cache = jnp.concatenate([key_rows, keyval_raw[:, HD:]], axis=1).astype(jnp.bfloat16)
    reach = min(WINDOW // tok_rows, seq_count - 1)

    def advance(counter, state):
        current, current_seg, store, store_seg = state
        current, current_seg = from_behind((current, current_seg), "seq", 1)
        slot = reach - 1 - counter
        store = lax.dynamic_update_slice_in_dim(store, current[None], slot, 0)
        store_seg = lax.dynamic_update_slice_in_dim(store_seg, current_seg[None], slot, 0)
        return (current, current_seg, store, store_seg)

    store_init = jnp.zeros((reach, tok_rows, kv_cache.shape[1]), jnp.bfloat16)
    seg_init = jnp.zeros((reach, tok_rows), jnp.int32)
    final_state = lax.fori_loop(0, reach, advance, (kv_cache, seg_ids, store_init, seg_init))
    block_kv = jnp.concatenate(
        [final_state[2].reshape(reach * tok_rows, kv_cache.shape[1]), kv_cache], axis=0
    )
    block_seg = jnp.concatenate([final_state[3].reshape(reach * tok_rows), seg_ids], axis=0)
    key_index = (my_index - reach) * tok_rows + jnp.arange((reach + 1) * tok_rows, dtype=jnp.int32)
    live = (block_seg[None, :] == seg_ids[:, None]) & (key_index[None, :] <= token_index[:, None])
    live = live & (token_index[:, None] - key_index[None, :] < WINDOW) & (key_index[None, :] >= 0)
    all_keys = block_kv[:, :HD]
    all_values = block_kv[:, HD:]
    head_outputs = []
    for head_idx in range(local_heads):
        scores = lax.dot_general(
            queries[:, head_idx, :],
            all_keys,
            (((1,), (1,)), ((), ())),
            preferred_element_type=jnp.float32,
        ) * HD ** (-0.5)
        scores = jnp.where(live, scores, -1e30)
        peak = jnp.max(scores, axis=1, keepdims=True)
        powered = jnp.exp(scores - peak)
        weights = (powered / jnp.sum(powered, axis=1, keepdims=True)).astype(jnp.bfloat16)
        head_outputs.append(
            jnp.dot(weights, all_values, preferred_element_type=jnp.float32).astype(jnp.bfloat16)
        )
    attended = jnp.concatenate(head_outputs, axis=1)
    partial_value = jnp.dot(
        attended,
        lax.all_gather(w_out, "seq", axis=1, tiled=True),
        preferred_element_type=jnp.float32,
    )
    summed = lax.psum_scatter(
        partial_value.astype(jnp.bfloat16), "tp", scatter_dimension=1, tiled=True
    ).astype(jnp.float32)
    hidden = (tokens.astype(jnp.float32) + summed).astype(jnp.bfloat16)
    return (hidden, kv_cache)


def solution(mesh):
    in_specs = (P("seq", "tp"), P("seq"), P(), P("seq", "tp"), P("seq", None), P("tp", "seq"))
    out_specs = (P("seq", "tp"), P("seq", None))
    return jax.shard_map(
        per_device, mesh=mesh, in_specs=in_specs, out_specs=out_specs, check_vma=False
    )
```

profile of v0, /device:TPU:2, one launch (start us, length us, event | category | flops | bytes accessed | tf_op | source)
XLA Modules:
  0.0 562.5 jit_solution(2328956909194726290)
XLA Ops:
  10.2 18.5 %all_gather.12 = bf16[128,2560]{1,0:T(8,128)(2,1)S(1)} all-gather(bf16[128,640]{1,0:T(8,128)(2,1)} %param.8), channel_id=1, replica_groups=mesh['seq'=128,'tp'=4] {'tp'}, dimensions={1}, use_global_device_ids=true | all-gather | bytes 819200 | tf_op jit(solution)/shard_map/all_gather | solution.py:45
  28.9 31.9 %psum.7 = s32[32]{0:T(128)S(1)} all-reduce(s32[32]{0:T(128)S(1)} %convert_reduce_fusion), channel_id=1, replica_groups=mesh['seq'=128,'tp'=4] {'seq'}, use_global_device_ids=true, to_apply=%region_2.0 | all-reduce | flops 32 | bytes 256 | tf_op jit(solution)/shard_map/psum | solution.py:50
  62.4 85.6 %all-gather.7.cloned.1.call-done = bf16[128,20,512]{2,1,0:T(8,128)(2,1)} async-done(((bf16[1,20,512]{2,1,0:T(8,128)(2,1)}), bf16[128,20,512]{2,1,0:T(8,128)(2,1)}) %all-gather.7.cloned.1.call-update) | async-done | bytes 2621456 | tf_op jit(solution)/shard_map/all_gather | solution.py:61
  148.0 3.6 reshape.164
  154.9 125.2 %all-gather.9.cloned.1.call-done = bf16[128,20,512]{2,1,0:T(8,128)(2,1)} async-done(((bf16[1,20,512]{2,1,0:T(8,128)(2,1)}), bf16[128,20,512]{2,1,0:T(8,128)(2,1)}) %all-gather.9.cloned.1.call-update) | async-done | bytes 2621456 | tf_op jit(solution)/shard_map/all_gather | solution.py:56
  280.1 3.6 reshape.166
  287.7 223.8 %while.19 = (s32[]{:T(128)}, bf16[128,512]{1,0:T(8,128)(2,1)S(1)}, s32[128]{0:T(128)S(1)}, bf16[16,128,512]{2,1,0:T(8,128)(2,1)S(1)}, s32[16,128]{1,0:T(8,128)S(...) while((s32[]{:T(128)}, bf16[128,512]{1,0:T(8,128)(2,1)S(1)}, s32[128]{0:T(128)S(1)}, ...), condition=%wide.region_5.6_spmd, body=%wide.region_4.5_spmd.sunk | while | flops 6 | bytes 1052899 | solution.py:80
  287.7 2.3 collective-permute-start
  289.9 2.4 collective-permute-start.1
  292.3 9.4 %collective-permute-done.1 = s32[128]{0:T(128)S(1)} collective-permute-done((s32[128]{0:T(128)S(1)}, s32[128]{0:T(128)S(1)}, u32[]{:S(2)}, u32[]{:S(2)}) %collective-permute-start.1) | collective-permute-done | bytes 544 | tf_op jit(solution)/shard_map/while/body/eval_jaxpr/ppermute | solution.py:14
  303.8 1.9 collective-permute-start.1
  305.7 9.9 %collective-permute-done.1 = s32[128]{0:T(128)S(1)} collective-permute-done((s32[128]{0:T(128)S(1)}, s32[128]{0:T(128)S(1)}, u32[]{:S(2)}, u32[]{:S(2)}) %collective-permute-start.1) | collective-permute-done | bytes 544 | tf_op jit(solution)/shard_map/while/body/eval_jaxpr/ppermute | solution.py:14
  315.7 1.9 collective-permute-start
  317.6 1.9 collective-permute-start.1
  319.6 10.9 %collective-permute-done.1 = s32[128]{0:T(128)S(1)} collective-permute-done((s32[128]{0:T(128)S(1)}, s32[128]{0:T(128)S(1)}, u32[]{:S(2)}, u32[]{:S(2)}) %collective-permute-start.1) | collective-permute-done | bytes 544 | tf_op jit(solution)/shard_map/while/body/eval_jaxpr/ppermute | solution.py:14
  334.5 9.9 %collective-permute-done.1 = s32[128]{0:T(128)S(1)} collective-permute-done((s32[128]{0:T(128)S(1)}, s32[128]{0:T(128)S(1)}, u32[]{:S(2)}, u32[]{:S(2)}) %collective-permute-start.1) | collective-permute-done | bytes 544 | tf_op jit(solution)/shard_map/while/body/eval_jaxpr/ppermute | solution.py:14
  348.3 9.9 %collective-permute-done.1 = s32[128]{0:T(128)S(1)} collective-permute-done((s32[128]{0:T(128)S(1)}, s32[128]{0:T(128)S(1)}, u32[]{:S(2)}, u32[]{:S(2)}) %collective-permute-start.1) | collective-permute-done | bytes 544 | tf_op jit(solution)/shard_map/while/body/eval_jaxpr/ppermute | solution.py:14
  362.1 9.9 %collective-permute-done.1 = s32[128]{0:T(128)S(1)} collective-permute-done((s32[128]{0:T(128)S(1)}, s32[128]{0:T(128)S(1)}, u32[]{:S(2)}, u32[]{:S(2)}) %collective-permute-start.1) | collective-permute-done | bytes 544 | tf_op jit(solution)/shard_map/while/body/eval_jaxpr/ppermute | solution.py:14
  375.9 9.9 %collective-permute-done.1 = s32[128]{0:T(128)S(1)} collective-permute-done((s32[128]{0:T(128)S(1)}, s32[128]{0:T(128)S(1)}, u32[]{:S(2)}, u32[]{:S(2)}) %collective-permute-start.1) | collective-permute-done | bytes 544 | tf_op jit(solution)/shard_map/while/body/eval_jaxpr/ppermute | solution.py:14
  386.0 1.9 collective-permute-start
  387.9 1.9 collective-permute-start.1
  389.8 11.0 %collective-permute-done.1 = s32[128]{0:T(128)S(1)} collective-permute-done((s32[128]{0:T(128)S(1)}, s32[128]{0:T(128)S(1)}, u32[]{:S(2)}, u32[]{:S(2)}) %collective-permute-start.1) | collective-permute-done | bytes 544 | tf_op jit(solution)/shard_map/while/body/eval_jaxpr/ppermute | solution.py:14
  404.8 9.9 %collective-permute-done.1 = s32[128]{0:T(128)S(1)} collective-permute-done((s32[128]{0:T(128)S(1)}, s32[128]{0:T(128)S(1)}, u32[]{:S(2)}, u32[]{:S(2)}) %collective-permute-start.1) | collective-permute-done | bytes 544 | tf_op jit(solution)/shard_map/while/body/eval_jaxpr/ppermute | solution.py:14
  418.6 9.9 %collective-permute-done.1 = s32[128]{0:T(128)S(1)} collective-permute-done((s32[128]{0:T(128)S(1)}, s32[128]{0:T(128)S(1)}, u32[]{:S(2)}, u32[]{:S(2)}) %collective-permute-start.1) | collective-permute-done | bytes 544 | tf_op jit(solution)/shard_map/while/body/eval_jaxpr/ppermute | solution.py:14
  432.4 9.9 %collective-permute-done.1 = s32[128]{0:T(128)S(1)} collective-permute-done((s32[128]{0:T(128)S(1)}, s32[128]{0:T(128)S(1)}, u32[]{:S(2)}, u32[]{:S(2)}) %collective-permute-start.1) | collective-permute-done | bytes 544 | tf_op jit(solution)/shard_map/while/body/eval_jaxpr/ppermute | solution.py:14
  446.2 9.9 %collective-permute-done.1 = s32[128]{0:T(128)S(1)} collective-permute-done((s32[128]{0:T(128)S(1)}, s32[128]{0:T(128)S(1)}, u32[]{:S(2)}, u32[]{:S(2)}) %collective-permute-start.1) | collective-permute-done | bytes 544 | tf_op jit(solution)/shard_map/while/body/eval_jaxpr/ppermute | solution.py:14
  460.1 9.9 %collective-permute-done.1 = s32[128]{0:T(128)S(1)} collective-permute-done((s32[128]{0:T(128)S(1)}, s32[128]{0:T(128)S(1)}, u32[]{:S(2)}, u32[]{:S(2)}) %collective-permute-start.1) | collective-permute-done | bytes 544 | tf_op jit(solution)/shard_map/while/body/eval_jaxpr/ppermute | solution.py:14
  473.9 9.9 %collective-permute-done.1 = s32[128]{0:T(128)S(1)} collective-permute-done((s32[128]{0:T(128)S(1)}, s32[128]{0:T(128)S(1)}, u32[]{:S(2)}, u32[]{:S(2)}) %collective-permute-start.1) | collective-permute-done | bytes 544 | tf_op jit(solution)/shard_map/while/body/eval_jaxpr/ppermute | solution.py:14
  487.7 9.9 %collective-permute-done.1 = s32[128]{0:T(128)S(1)} collective-permute-done((s32[128]{0:T(128)S(1)}, s32[128]{0:T(128)S(1)}, u32[]{:S(2)}, u32[]{:S(2)}) %collective-permute-start.1) | collective-permute-done | bytes 544 | tf_op jit(solution)/shard_map/while/body/eval_jaxpr/ppermute | solution.py:14
  501.5 9.9 %collective-permute-done.1 = s32[128]{0:T(128)S(1)} collective-permute-done((s32[128]{0:T(128)S(1)}, s32[128]{0:T(128)S(1)}, u32[]{:S(2)}, u32[]{:S(2)}) %collective-permute-start.1) | collective-permute-done | bytes 544 | tf_op jit(solution)/shard_map/while/body/eval_jaxpr/ppermute | solution.py:14
  515.1 3.6 reshape.168
  520.9 33.3 %reduce-scatter.4.cloned.1.call-done = bf16[640,128]{1,0:T(8,128)(2,1)} async-done(((bf16[2560,128]{1,0:T(8,128)(2,1)}), bf16[640,128]{1,0:T(8,128)(2,1)}) %reduce-scatter.4.cloned.1.call-update) | async-done | bytes 163856
  (173 shorter events, 68.2 us)
Async XLA Ops:
  7.2 140.8 %all-gather.7.cloned.1.call-start = ((), (), s32[]{:S(2)}) async-start(), calls=%async_computation.1 | async-start | bytes 3170304 | tf_op jit(solution)/shard_map/all_gather | solution.py:61
  7.9 272.1 %all-gather.9.cloned.1.call-start = ((), (), s32[]{:S(2)}) async-start(), calls=%async_computation.2 | async-start | bytes 3170304 | tf_op jit(solution)/shard_map/all_gather | solution.py:56
  8.7 506.4 %all-gather.11.cloned.1.call-start = ((), (), s32[]{:S(2)}) async-start(), calls=%async_computation.3 | async-start | bytes 3170304 | tf_op jit(solution)/shard_map/all_gather | solution.py:108
  9.4 544.8 %reduce-scatter.4.cloned.1.call-start = ((), (), s32[]{:S(2)}) async-start(), calls=%async_computation.4 | async-start | bytes 819200
  287.7 14.1 %collective-permute-start = (bf16[128,512]{1,0:T(8,128)(2,1)S(1)}, bf16[128,512]{1,0:T(8,128)(2,1)S(1)}, u32[]{:S(2)}, u32[]{:S(2)}) collective-permute-start(bf16[128,512]{1,0:T(8,128)(2,1)S(1)} %get-tuple-element.171), channel_id=1, source_target_pairs={{0,4},{4,8},{8,12},{12,16},{16,20},{20,24},{24,28},{28,32},{32,36}... | collective-permute-start | bytes 393224 | tf_op jit(solution)/shard_map/while/body/eval_jaxpr/ppermute | solution.py:14
  289.9 11.8 %collective-permute-start.1 = (s32[128]{0:T(128)S(1)}, s32[128]{0:T(128)S(1)}, u32[]{:S(2)}, u32[]{:S(2)}) collective-permute-start(s32[128]{0:T(128)S(1)} %get-tuple-element.172), channel_id=1, source_target_pairs={{0,4},{4,8},{8,12},{12,16},{16,20},{20,24},{24,28},{28,32},{32,36}... | collective-permute-start | bytes 1544 | tf_op jit(solution)/shard_map/while/body/eval_jaxpr/ppermute | solution.py:14
  301.8 13.8 %collective-permute-start = (bf16[128,512]{1,0:T(8,128)(2,1)S(1)}, bf16[128,512]{1,0:T(8,128)(2,1)S(1)}, u32[]{:S(2)}, u32[]{:S(2)}) collective-permute-start(bf16[128,512]{1,0:T(8,128)(2,1)S(1)} %get-tuple-element.171), channel_id=1, source_target_pairs={{0,4},{4,8},{8,12},{12,16},{16,20},{20,24},{24,28},{28,32},{32,36}... | collective-permute-start | bytes 393224 | tf_op jit(solution)/shard_map/while/body/eval_jaxpr/ppermute | solution.py:14
  303.8 11.9 %collective-permute-start.1 = (s32[128]{0:T(128)S(1)}, s32[128]{0:T(128)S(1)}, u32[]{:S(2)}, u32[]{:S(2)}) collective-permute-start(s32[128]{0:T(128)S(1)} %get-tuple-element.172), channel_id=1, source_target_pairs={{0,4},{4,8},{8,12},{12,16},{16,20},{20,24},{24,28},{28,32},{32,36}... | collective-permute-start | bytes 1544 | tf_op jit(solution)/shard_map/while/body/eval_jaxpr/ppermute | solution.py:14
  315.7 14.8 %collective-permute-start = (bf16[128,512]{1,0:T(8,128)(2,1)S(1)}, bf16[128,512]{1,0:T(8,128)(2,1)S(1)}, u32[]{:S(2)}, u32[]{:S(2)}) collective-permute-start(bf16[128,512]{1,0:T(8,128)(2,1)S(1)} %get-tuple-element.171), channel_id=1, source_target_pairs={{0,4},{4,8},{8,12},{12,16},{16,20},{20,24},{24,28},{28,32},{32,36}... | collective-permute-start | bytes 393224 | tf_op jit(solution)/shard_map/while/body/eval_jaxpr/ppermute | solution.py:14
  317.6 12.9 %collective-permute-start.1 = (s32[128]{0:T(128)S(1)}, s32[128]{0:T(128)S(1)}, u32[]{:S(2)}, u32[]{:S(2)}) collective-permute-start(s32[128]{0:T(128)S(1)} %get-tuple-element.172), channel_id=1, source_target_pairs={{0,4},{4,8},{8,12},{12,16},{16,20},{20,24},{24,28},{28,32},{32,36}... | collective-permute-start | bytes 1544 | tf_op jit(solution)/shard_map/while/body/eval_jaxpr/ppermute | solution.py:14
  330.6 13.8 %collective-permute-start = (bf16[128,512]{1,0:T(8,128)(2,1)S(1)}, bf16[128,512]{1,0:T(8,128)(2,1)S(1)}, u32[]{:S(2)}, u32[]{:S(2)}) collective-permute-start(bf16[128,512]{1,0:T(8,128)(2,1)S(1)} %get-tuple-element.171), channel_id=1, source_target_pairs={{0,4},{4,8},{8,12},{12,16},{16,20},{20,24},{24,28},{28,32},{32,36}... | collective-permute-start | bytes 393224 | tf_op jit(solution)/shard_map/while/body/eval_jaxpr/ppermute | solution.py:14
  332.5 11.8 %collective-permute-start.1 = (s32[128]{0:T(128)S(1)}, s32[128]{0:T(128)S(1)}, u32[]{:S(2)}, u32[]{:S(2)}) collective-permute-start(s32[128]{0:T(128)S(1)} %get-tuple-element.172), channel_id=1, source_target_pairs={{0,4},{4,8},{8,12},{12,16},{16,20},{20,24},{24,28},{28,32},{32,36}... | collective-permute-start | bytes 1544 | tf_op jit(solution)/shard_map/while/body/eval_jaxpr/ppermute | solution.py:14
  344.4 13.8 %collective-permute-start = (bf16[128,512]{1,0:T(8,128)(2,1)S(1)}, bf16[128,512]{1,0:T(8,128)(2,1)S(1)}, u32[]{:S(2)}, u32[]{:S(2)}) collective-permute-start(bf16[128,512]{1,0:T(8,128)(2,1)S(1)} %get-tuple-element.171), channel_id=1, source_target_pairs={{0,4},{4,8},{8,12},{12,16},{16,20},{20,24},{24,28},{28,32},{32,36}... | collective-permute-start | bytes 393224 | tf_op jit(solution)/shard_map/while/body/eval_jaxpr/ppermute | solution.py:14
  346.4 11.8 %collective-permute-start.1 = (s32[128]{0:T(128)S(1)}, s32[128]{0:T(128)S(1)}, u32[]{:S(2)}, u32[]{:S(2)}) collective-permute-start(s32[128]{0:T(128)S(1)} %get-tuple-element.172), channel_id=1, source_target_pairs={{0,4},{4,8},{8,12},{12,16},{16,20},{20,24},{24,28},{28,32},{32,36}... | collective-permute-start | bytes 1544 | tf_op jit(solution)/shard_map/while/body/eval_jaxpr/ppermute | solution.py:14
  358.3 13.8 %collective-permute-start = (bf16[128,512]{1,0:T(8,128)(2,1)S(1)}, bf16[128,512]{1,0:T(8,128)(2,1)S(1)}, u32[]{:S(2)}, u32[]{:S(2)}) collective-permute-start(bf16[128,512]{1,0:T(8,128)(2,1)S(1)} %get-tuple-element.171), channel_id=1, source_target_pairs={{0,4},{4,8},{8,12},{12,16},{16,20},{20,24},{24,28},{28,32},{32,36}... | collective-permute-start | bytes 393224 | tf_op jit(solution)/shard_map/while/body/eval_jaxpr/ppermute | solution.py:14
  360.2 11.8 %collective-permute-start.1 = (s32[128]{0:T(128)S(1)}, s32[128]{0:T(128)S(1)}, u32[]{:S(2)}, u32[]{:S(2)}) collective-permute-start(s32[128]{0:T(128)S(1)} %get-tuple-element.172), channel_id=1, source_target_pairs={{0,4},{4,8},{8,12},{12,16},{16,20},{20,24},{24,28},{28,32},{32,36}... | collective-permute-start | bytes 1544 | tf_op jit(solution)/shard_map/while/body/eval_jaxpr/ppermute | solution.py:14
  372.1 13.8 %collective-permute-start = (bf16[128,512]{1,0:T(8,128)(2,1)S(1)}, bf16[128,512]{1,0:T(8,128)(2,1)S(1)}, u32[]{:S(2)}, u32[]{:S(2)}) collective-permute-start(bf16[128,512]{1,0:T(8,128)(2,1)S(1)} %get-tuple-element.171), channel_id=1, source_target_pairs={{0,4},{4,8},{8,12},{12,16},{16,20},{20,24},{24,28},{28,32},{32,36}... | collective-permute-start | bytes 393224 | tf_op jit(solution)/shard_map/while/body/eval_jaxpr/ppermute | solution.py:14
  374.0 11.9 %collective-permute-start.1 = (s32[128]{0:T(128)S(1)}, s32[128]{0:T(128)S(1)}, u32[]{:S(2)}, u32[]{:S(2)}) collective-permute-start(s32[128]{0:T(128)S(1)} %get-tuple-element.172), channel_id=1, source_target_pairs={{0,4},{4,8},{8,12},{12,16},{16,20},{20,24},{24,28},{28,32},{32,36}... | collective-permute-start | bytes 1544 | tf_op jit(solution)/shard_map/while/body/eval_jaxpr/ppermute | solution.py:14
  386.0 14.9 %collective-permute-start = (bf16[128,512]{1,0:T(8,128)(2,1)S(1)}, bf16[128,512]{1,0:T(8,128)(2,1)S(1)}, u32[]{:S(2)}, u32[]{:S(2)}) collective-permute-start(bf16[128,512]{1,0:T(8,128)(2,1)S(1)} %get-tuple-element.171), channel_id=1, source_target_pairs={{0,4},{4,8},{8,12},{12,16},{16,20},{20,24},{24,28},{28,32},{32,36}... | collective-permute-start | bytes 393224 | tf_op jit(solution)/shard_map/while/body/eval_jaxpr/ppermute | solution.py:14
  387.9 12.9 %collective-permute-start.1 = (s32[128]{0:T(128)S(1)}, s32[128]{0:T(128)S(1)}, u32[]{:S(2)}, u32[]{:S(2)}) collective-permute-start(s32[128]{0:T(128)S(1)} %get-tuple-element.172), channel_id=1, source_target_pairs={{0,4},{4,8},{8,12},{12,16},{16,20},{20,24},{24,28},{28,32},{32,36}... | collective-permute-start | bytes 1544 | tf_op jit(solution)/shard_map/while/body/eval_jaxpr/ppermute | solution.py:14
  400.9 13.8 %collective-permute-start = (bf16[128,512]{1,0:T(8,128)(2,1)S(1)}, bf16[128,512]{1,0:T(8,128)(2,1)S(1)}, u32[]{:S(2)}, u32[]{:S(2)}) collective-permute-start(bf16[128,512]{1,0:T(8,128)(2,1)S(1)} %get-tuple-element.171), channel_id=1, source_target_pairs={{0,4},{4,8},{8,12},{12,16},{16,20},{20,24},{24,28},{28,32},{32,36}... | collective-permute-start | bytes 393224 | tf_op jit(solution)/shard_map/while/body/eval_jaxpr/ppermute | solution.py:14
  402.8 11.8 %collective-permute-start.1 = (s32[128]{0:T(128)S(1)}, s32[128]{0:T(128)S(1)}, u32[]{:S(2)}, u32[]{:S(2)}) collective-permute-start(s32[128]{0:T(128)S(1)} %get-tuple-element.172), channel_id=1, source_target_pairs={{0,4},{4,8},{8,12},{12,16},{16,20},{20,24},{24,28},{28,32},{32,36}... | collective-permute-start | bytes 1544 | tf_op jit(solution)/shard_map/while/body/eval_jaxpr/ppermute | solution.py:14
  414.7 13.8 %collective-permute-start = (bf16[128,512]{1,0:T(8,128)(2,1)S(1)}, bf16[128,512]{1,0:T(8,128)(2,1)S(1)}, u32[]{:S(2)}, u32[]{:S(2)}) collective-permute-start(bf16[128,512]{1,0:T(8,128)(2,1)S(1)} %get-tuple-element.171), channel_id=1, source_target_pairs={{0,4},{4,8},{8,12},{12,16},{16,20},{20,24},{24,28},{28,32},{32,36}... | collective-permute-start | bytes 393224 | tf_op jit(solution)/shard_map/while/body/eval_jaxpr/ppermute | solution.py:14
  416.7 11.8 %collective-permute-start.1 = (s32[128]{0:T(128)S(1)}, s32[128]{0:T(128)S(1)}, u32[]{:S(2)}, u32[]{:S(2)}) collective-permute-start(s32[128]{0:T(128)S(1)} %get-tuple-element.172), channel_id=1, source_target_pairs={{0,4},{4,8},{8,12},{12,16},{16,20},{20,24},{24,28},{28,32},{32,36}... | collective-permute-start | bytes 1544 | tf_op jit(solution)/shard_map/while/body/eval_jaxpr/ppermute | solution.py:14
  428.6 13.8 %collective-permute-start = (bf16[128,512]{1,0:T(8,128)(2,1)S(1)}, bf16[128,512]{1,0:T(8,128)(2,1)S(1)}, u32[]{:S(2)}, u32[]{:S(2)}) collective-permute-start(bf16[128,512]{1,0:T(8,128)(2,1)S(1)} %get-tuple-element.171), channel_id=1, source_target_pairs={{0,4},{4,8},{8,12},{12,16},{16,20},{20,24},{24,28},{28,32},{32,36}... | collective-permute-start | bytes 393224 | tf_op jit(solution)/shard_map/while/body/eval_jaxpr/ppermute | solution.py:14
  430.5 11.8 %collective-permute-start.1 = (s32[128]{0:T(128)S(1)}, s32[128]{0:T(128)S(1)}, u32[]{:S(2)}, u32[]{:S(2)}) collective-permute-start(s32[128]{0:T(128)S(1)} %get-tuple-element.172), channel_id=1, source_target_pairs={{0,4},{4,8},{8,12},{12,16},{16,20},{20,24},{24,28},{28,32},{32,36}... | collective-permute-start | bytes 1544 | tf_op jit(solution)/shard_map/while/body/eval_jaxpr/ppermute | solution.py:14
  442.4 13.8 %collective-permute-start = (bf16[128,512]{1,0:T(8,128)(2,1)S(1)}, bf16[128,512]{1,0:T(8,128)(2,1)S(1)}, u32[]{:S(2)}, u32[]{:S(2)}) collective-permute-start(bf16[128,512]{1,0:T(8,128)(2,1)S(1)} %get-tuple-element.171), channel_id=1, source_target_pairs={{0,4},{4,8},{8,12},{12,16},{16,20},{20,24},{24,28},{28,32},{32,36}... | collective-permute-start | bytes 393224 | tf_op jit(solution)/shard_map/while/body/eval_jaxpr/ppermute | solution.py:14
  456.2 13.8 %collective-permute-start = (bf16[128,512]{1,0:T(8,128)(2,1)S(1)}, bf16[128,512]{1,0:T(8,128)(2,1)S(1)}, u32[]{:S(2)}, u32[]{:S(2)}) collective-permute-start(bf16[128,512]{1,0:T(8,128)(2,1)S(1)} %get-tuple-element.171), channel_id=1, source_target_pairs={{0,4},{4,8},{8,12},{12,16},{16,20},{20,24},{24,28},{28,32},{32,36}... | collective-permute-start | bytes 393224 | tf_op jit(solution)/shard_map/while/body/eval_jaxpr/ppermute | solution.py:14
  470.0 13.8 %collective-permute-start = (bf16[128,512]{1,0:T(8,128)(2,1)S(1)}, bf16[128,512]{1,0:T(8,128)(2,1)S(1)}, u32[]{:S(2)}, u32[]{:S(2)}) collective-permute-start(bf16[128,512]{1,0:T(8,128)(2,1)S(1)} %get-tuple-element.171), channel_id=1, source_target_pairs={{0,4},{4,8},{8,12},{12,16},{16,20},{20,24},{24,28},{28,32},{32,36}... | collective-permute-start | bytes 393224 | tf_op jit(solution)/shard_map/while/body/eval_jaxpr/ppermute | solution.py:14
  483.9 13.8 %collective-permute-start = (bf16[128,512]{1,0:T(8,128)(2,1)S(1)}, bf16[128,512]{1,0:T(8,128)(2,1)S(1)}, u32[]{:S(2)}, u32[]{:S(2)}) collective-permute-start(bf16[128,512]{1,0:T(8,128)(2,1)S(1)} %get-tuple-element.171), channel_id=1, source_target_pairs={{0,4},{4,8},{8,12},{12,16},{16,20},{20,24},{24,28},{28,32},{32,36}... | collective-permute-start | bytes 393224 | tf_op jit(solution)/shard_map/while/body/eval_jaxpr/ppermute | solution.py:14
  485.8 11.8 %collective-permute-start.1 = (s32[128]{0:T(128)S(1)}, s32[128]{0:T(128)S(1)}, u32[]{:S(2)}, u32[]{:S(2)}) collective-permute-start(s32[128]{0:T(128)S(1)} %get-tuple-element.172), channel_id=1, source_target_pairs={{0,4},{4,8},{8,12},{12,16},{16,20},{20,24},{24,28},{28,32},{32,36}... | collective-permute-start | bytes 1544 | tf_op jit(solution)/shard_map/while/body/eval_jaxpr/ppermute | solution.py:14
  497.7 13.8 %collective-permute-start = (bf16[128,512]{1,0:T(8,128)(2,1)S(1)}, bf16[128,512]{1,0:T(8,128)(2,1)S(1)}, u32[]{:S(2)}, u32[]{:S(2)}) collective-permute-start(bf16[128,512]{1,0:T(8,128)(2,1)S(1)} %get-tuple-element.171), channel_id=1, source_target_pairs={{0,4},{4,8},{8,12},{12,16},{16,20},{20,24},{24,28},{28,32},{32,36}... | collective-permute-start | bytes 393224 | tf_op jit(solution)/shard_map/while/body/eval_jaxpr/ppermute | solution.py:14
  (14 other events, 1181.9 us)
Sparse Core Ops, SparseCore 0:
  12.7 135.2 all-gather.6
  152.7 127.3 all-gather.8
  284.8 126.9 all-gather.10
  521.0 33.1 reduce-scatter.3
where the time goes:
time: 564 us; the launch traced here: 562 us
  waiting for transfers between devices  406 us (72%)
  starting transfers between devices  62.4 us (11%)
  blocking collectives  50.3 us (9%)
  local copies, waits for them, and re-layouts  16.6 us (3%)
  between operations  14.1 us (2%)
  other arithmetic  6.51 us (1%)
  matrix products  5.67 us (1%)
    ppermute x32, waiting for transfers between devices, from_behind(): return lax.ppermute(x, axis, pairs)  160 us
    all_gather x1, waiting for transfers between devices, per_device(): lax.all_gather(w_query, 'seq', axis=0, tiled=True)  125 us
    all_gather x1, waiting for transfers between devices, per_device(): lax.all_gather(w_keyval, 'seq', axis=0, tiled=True)  85.6 us
    ppermute x32, starting transfers between devices, from_behind(): return lax.ppermute(x, axis, pairs)  62.3 us
    unnamed x5, waiting for transfers between devices  35.4 us
    psum x1, blocking collectives, per_device(): starts = lax.psum(below, 'seq')  31.9 us
    all_gather x1, blocking collectives, per_device(): gathered = lax.all_gather(tokens, 'tp', axis=1, tiled=True)  18.5 us
    unnamed x27, local copies, waits for them, and re-layouts  13.8 us
  transfers between devices with their start and end apart: 36, of which 19 were waited for; matrix products, arithmetic and copies ran while one was open for 4% of the time, Pallas kernels for 0%

commit v1 on v0

--- a/solution.py
+++ b/solution.py
@@ -47,7 +47,7 @@
     seg_total = tok_rows * seq_count // SEG_MEAN
     labels = jnp.arange(seg_total, dtype=jnp.int32)
     below = jnp.sum((seg_ids[None, :] < labels[:, None]).astype(jnp.int32), axis=1)
-    starts = lax.psum(below, "seq")
+    starts = jnp.sum(lax.all_gather(below, "seq"), axis=0)
     own_start = jnp.sum(jnp.where(seg_ids[:, None] == labels[None, :], starts[None, :], 0), axis=1)
     token_index = my_index * tok_rows + jnp.arange(tok_rows, dtype=jnp.int32)
     positions = (token_index - own_start).astype(jnp.float32)

time: 564 us -> 1060 us (1.88)
  blocking collectives: 50.3 us -> 755 us
  waiting for transfers between devices: 406 us -> 193 us
    unnamed x0 -> x1, blocking collectives: none -> 737 us
    all_gather x1, waiting for transfers between devices: 125 us -> 0.01 us  [per_device(): lax.all_gather(w_query, 'seq', axis=0, tiled=True)]
    all_gather x1, waiting for transfers between devices: 85.6 us -> 0.01 us  [per_device(): lax.all_gather(w_keyval, 'seq', axis=0, tiled=True)]
    psum x1 -> x0, blocking collectives: 31.9 us -> none  [per_device(): starts = lax.psum(below, 'seq')]
  transfers between devices with their start and end apart: 36 -> 36, of which waited for: 19 -> 17; matrix products, arithmetic and copies ran while one was open for 4% -> 2% of each run, Pallas kernels for 0% -> 0%
where the time goes in v1:
time: 1060 us
  blocking collectives  755 us (71%)
  waiting for transfers between devices  193 us (18%)
  starting transfers between devices  61.7 us (6%)
  local copies, waits for them, and re-layouts  18.3 us (2%)
  between operations  14.7 us (1%)
    unnamed x1, blocking collectives  737 us
    ppermute x32, waiting for transfers between devices, from_behind(): return lax.ppermute(x, axis, pairs)  159 us
    ppermute x32, starting transfers between devices, from_behind(): return lax.ppermute(x, axis, pairs)  61.6 us
    unnamed x5, waiting for transfers between devices  33.9 us
  transfers between devices with their start and end apart: 36, of which 17 were waited for; matrix products, arithmetic and copies ran while one was open for 2% of the time, Pallas kernels for 0%

profile of v1, /device:TPU:2, one launch (start us, length us, event | category | flops | bytes accessed | tf_op | source)
XLA Modules:
  0.0 1055.9 jit_solution(931985239734382381)
XLA Ops:
  10.2 18.5 %all_gather.18 = bf16[128,2560]{1,0:T(8,128)(2,1)S(1)} all-gather(bf16[128,640]{1,0:T(8,128)(2,1)} %param.8), channel_id=1, replica_groups=mesh['seq'=128,'tp'=4] {'tp'}, dimensions={1}, use_global_device_ids=true | all-gather | bytes 819200 | tf_op jit(solution)/shard_map/all_gather | solution.py:45
  31.2 736.5 %all-reduce = s32[4096]{0:T(1024)S(1)} all-reduce(s32[4096]{0:T(1024)S(1)} %dynamic-update-slice), channel_id=2, replica_groups=mesh['seq'=128,'tp'=4] {'seq'}, use_global_device_ids=true, to_apply=%add | all-reduce | flops 4096 | bytes 32768
  769.5 3.6 reshape.168
  776.4 3.6 reshape.170
  784.0 222.3 %while.19 = (s32[]{:T(128)}, bf16[128,512]{1,0:T(8,128)(2,1)S(1)}, s32[128]{0:T(128)S(1)}, bf16[16,128,512]{2,1,0:T(8,128)(2,1)S(1)}, s32[16,128]{1,0:T(8,128)S(...) while((s32[]{:T(128)}, bf16[128,512]{1,0:T(8,128)(2,1)S(1)}, s32[128]{0:T(128)S(1)}, ...), condition=%wide.region_5.6_spmd, body=%wide.region_4.5_spmd.sunk | while | flops 6 | bytes 1052899 | solution.py:80
  784.0 2.0 collective-permute-start
  786.0 1.9 collective-permute-start.1
  787.9 9.9 collective-permute-done.1
  801.8 9.9 collective-permute-done.1
  811.7 1.9 collective-permute-start
  813.7 1.9 collective-permute-start.1
  815.6 9.9 collective-permute-done.1
  829.4 9.9 collective-permute-done.1
  839.4 1.9 collective-permute-start
  843.2 9.9 collective-permute-done.1
  857.1 9.9 collective-permute-done.1
  870.9 9.9 collective-permute-done.1
  884.8 10.8 %collective-permute-done.1 = s32[128]{0:T(128)S(1)} collective-permute-done((s32[128]{0:T(128)S(1)}, s32[128]{0:T(128)S(1)}, u32[]{:S(2)}, u32[]{:S(2)}) %collective-permute-start.1) | collective-permute-done | bytes 544 | tf_op jit(solution)/shard_map/while/body/eval_jaxpr/ppermute | solution.py:14
  895.7 1.9 collective-permute-start
  897.6 1.9 collective-permute-start.1
  899.6 9.9 collective-permute-done.1
  913.4 9.9 collective-permute-done.1
  923.3 1.9 collective-permute-start
  925.3 1.9 collective-permute-start.1
  927.2 9.9 collective-permute-done.1
  941.0 9.9 collective-permute-done.1
  954.9 9.9 collective-permute-done.1
  968.7 9.9 collective-permute-done.1
  982.5 9.9 collective-permute-done.1
  996.3 9.9 collective-permute-done.1
  1010.0 3.6 reshape.172
  1015.7 31.8 %reduce-scatter.4.cloned.1.call-done = bf16[640,128]{1,0:T(8,128)(2,1)} async-done(((bf16[2560,128]{1,0:T(8,128)(2,1)}), bf16[640,128]{1,0:T(8,128)(2,1)}) %reduce-scatter.4.cloned.1.call-update) | async-done | bytes 163856
  (178 shorter events, 66.2 us)
Async XLA Ops:
  7.2 762.3 %all-gather.8.cloned.1.call-start = ((), (), s32[]{:S(2)}) async-start(), calls=%async_computation.1 | async-start | bytes 3170304 | tf_op jit(solution)/shard_map/all_gather | solution.py:61
  7.9 768.5 %all-gather.10.cloned.1.call-start = ((), (), s32[]{:S(2)}) async-start(), calls=%async_computation.2 | async-start | bytes 3170304 | tf_op jit(solution)/shard_map/all_gather | solution.py:56
  8.7 1001.3 %all-gather.12.cloned.1.call-start = ((), (), s32[]{:S(2)}) async-start(), calls=%async_computation.3 | async-start | bytes 3170304 | tf_op jit(solution)/shard_map/all_gather | solution.py:108
  9.4 1038.1 %reduce-scatter.4.cloned.1.call-start = ((), (), s32[]{:S(2)}) async-start(), calls=%async_computation.4 | async-start | bytes 819200
  784.0 13.9 %collective-permute-start = (bf16[128,512]{1,0:T(8,128)(2,1)S(1)}, bf16[128,512]{1,0:T(8,128)(2,1)S(1)}, u32[]{:S(2)}, u32[]{:S(2)}) collective-permute-start(bf16[128,512]{1,0:T(8,128)(2,1)S(1)} %get-tuple-element.171), channel_id=1, source_target_pairs={{0,4},{4,8},{8,12},{12,16},{16,20},{20,24},{24,28},{28,32},{32,36}... | collective-permute-start | bytes 393224 | tf_op jit(solution)/shard_map/while/body/eval_jaxpr/ppermute | solution.py:14
  786.0 11.8 %collective-permute-start.1 = (s32[128]{0:T(128)S(1)}, s32[128]{0:T(128)S(1)}, u32[]{:S(2)}, u32[]{:S(2)}) collective-permute-start(s32[128]{0:T(128)S(1)} %get-tuple-element.172), channel_id=1, source_target_pairs={{0,4},{4,8},{8,12},{12,16},{16,20},{20,24},{24,28},{28,32},{32,36}... | collective-permute-start | bytes 1544 | tf_op jit(solution)/shard_map/while/body/eval_jaxpr/ppermute | solution.py:14
  797.9 13.8 %collective-permute-start = (bf16[128,512]{1,0:T(8,128)(2,1)S(1)}, bf16[128,512]{1,0:T(8,128)(2,1)S(1)}, u32[]{:S(2)}, u32[]{:S(2)}) collective-permute-start(bf16[128,512]{1,0:T(8,128)(2,1)S(1)} %get-tuple-element.171), channel_id=1, source_target_pairs={{0,4},{4,8},{8,12},{12,16},{16,20},{20,24},{24,28},{28,32},{32,36}... | collective-permute-start | bytes 393224 | tf_op jit(solution)/shard_map/while/body/eval_jaxpr/ppermute | solution.py:14
  799.8 11.8 %collective-permute-start.1 = (s32[128]{0:T(128)S(1)}, s32[128]{0:T(128)S(1)}, u32[]{:S(2)}, u32[]{:S(2)}) collective-permute-start(s32[128]{0:T(128)S(1)} %get-tuple-element.172), channel_id=1, source_target_pairs={{0,4},{4,8},{8,12},{12,16},{16,20},{20,24},{24,28},{28,32},{32,36}... | collective-permute-start | bytes 1544 | tf_op jit(solution)/shard_map/while/body/eval_jaxpr/ppermute | solution.py:14
  811.7 13.8 %collective-permute-start = (bf16[128,512]{1,0:T(8,128)(2,1)S(1)}, bf16[128,512]{1,0:T(8,128)(2,1)S(1)}, u32[]{:S(2)}, u32[]{:S(2)}) collective-permute-start(bf16[128,512]{1,0:T(8,128)(2,1)S(1)} %get-tuple-element.171), channel_id=1, source_target_pairs={{0,4},{4,8},{8,12},{12,16},{16,20},{20,24},{24,28},{28,32},{32,36}... | collective-permute-start | bytes 393224 | tf_op jit(solution)/shard_map/while/body/eval_jaxpr/ppermute | solution.py:14
  813.7 11.8 %collective-permute-start.1 = (s32[128]{0:T(128)S(1)}, s32[128]{0:T(128)S(1)}, u32[]{:S(2)}, u32[]{:S(2)}) collective-permute-start(s32[128]{0:T(128)S(1)} %get-tuple-element.172), channel_id=1, source_target_pairs={{0,4},{4,8},{8,12},{12,16},{16,20},{20,24},{24,28},{28,32},{32,36}... | collective-permute-start | bytes 1544 | tf_op jit(solution)/shard_map/while/body/eval_jaxpr/ppermute | solution.py:14
  825.6 13.8 %collective-permute-start = (bf16[128,512]{1,0:T(8,128)(2,1)S(1)}, bf16[128,512]{1,0:T(8,128)(2,1)S(1)}, u32[]{:S(2)}, u32[]{:S(2)}) collective-permute-start(bf16[128,512]{1,0:T(8,128)(2,1)S(1)} %get-tuple-element.171), channel_id=1, source_target_pairs={{0,4},{4,8},{8,12},{12,16},{16,20},{20,24},{24,28},{28,32},{32,36}... | collective-permute-start | bytes 393224 | tf_op jit(solution)/shard_map/while/body/eval_jaxpr/ppermute | solution.py:14
  827.5 11.8 %collective-permute-start.1 = (s32[128]{0:T(128)S(1)}, s32[128]{0:T(128)S(1)}, u32[]{:S(2)}, u32[]{:S(2)}) collective-permute-start(s32[128]{0:T(128)S(1)} %get-tuple-element.172), channel_id=1, source_target_pairs={{0,4},{4,8},{8,12},{12,16},{16,20},{20,24},{24,28},{28,32},{32,36}... | collective-permute-start | bytes 1544 | tf_op jit(solution)/shard_map/while/body/eval_jaxpr/ppermute | solution.py:14
  839.4 13.8 %collective-permute-start = (bf16[128,512]{1,0:T(8,128)(2,1)S(1)}, bf16[128,512]{1,0:T(8,128)(2,1)S(1)}, u32[]{:S(2)}, u32[]{:S(2)}) collective-permute-start(bf16[128,512]{1,0:T(8,128)(2,1)S(1)} %get-tuple-element.171), channel_id=1, source_target_pairs={{0,4},{4,8},{8,12},{12,16},{16,20},{20,24},{24,28},{28,32},{32,36}... | collective-permute-start | bytes 393224 | tf_op jit(solution)/shard_map/while/body/eval_jaxpr/ppermute | solution.py:14
  841.3 11.8 %collective-permute-start.1 = (s32[128]{0:T(128)S(1)}, s32[128]{0:T(128)S(1)}, u32[]{:S(2)}, u32[]{:S(2)}) collective-permute-start(s32[128]{0:T(128)S(1)} %get-tuple-element.172), channel_id=1, source_target_pairs={{0,4},{4,8},{8,12},{12,16},{16,20},{20,24},{24,28},{28,32},{32,36}... | collective-permute-start | bytes 1544 | tf_op jit(solution)/shard_map/while/body/eval_jaxpr/ppermute | solution.py:14
  853.2 13.8 %collective-permute-start = (bf16[128,512]{1,0:T(8,128)(2,1)S(1)}, bf16[128,512]{1,0:T(8,128)(2,1)S(1)}, u32[]{:S(2)}, u32[]{:S(2)}) collective-permute-start(bf16[128,512]{1,0:T(8,128)(2,1)S(1)} %get-tuple-element.171), channel_id=1, source_target_pairs={{0,4},{4,8},{8,12},{12,16},{16,20},{20,24},{24,28},{28,32},{32,36}... | collective-permute-start | bytes 393224 | tf_op jit(solution)/shard_map/while/body/eval_jaxpr/ppermute | solution.py:14
  855.1 11.8 %collective-permute-start.1 = (s32[128]{0:T(128)S(1)}, s32[128]{0:T(128)S(1)}, u32[]{:S(2)}, u32[]{:S(2)}) collective-permute-start(s32[128]{0:T(128)S(1)} %get-tuple-element.172), channel_id=1, source_target_pairs={{0,4},{4,8},{8,12},{12,16},{16,20},{20,24},{24,28},{28,32},{32,36}... | collective-permute-start | bytes 1544 | tf_op jit(solution)/shard_map/while/body/eval_jaxpr/ppermute | solution.py:14
  867.0 13.8 %collective-permute-start = (bf16[128,512]{1,0:T(8,128)(2,1)S(1)}, bf16[128,512]{1,0:T(8,128)(2,1)S(1)}, u32[]{:S(2)}, u32[]{:S(2)}) collective-permute-start(bf16[128,512]{1,0:T(8,128)(2,1)S(1)} %get-tuple-element.171), channel_id=1, source_target_pairs={{0,4},{4,8},{8,12},{12,16},{16,20},{20,24},{24,28},{28,32},{32,36}... | collective-permute-start | bytes 393224 | tf_op jit(solution)/shard_map/while/body/eval_jaxpr/ppermute | solution.py:14
  869.0 11.9 %collective-permute-start.1 = (s32[128]{0:T(128)S(1)}, s32[128]{0:T(128)S(1)}, u32[]{:S(2)}, u32[]{:S(2)}) collective-permute-start(s32[128]{0:T(128)S(1)} %get-tuple-element.172), channel_id=1, source_target_pairs={{0,4},{4,8},{8,12},{12,16},{16,20},{20,24},{24,28},{28,32},{32,36}... | collective-permute-start | bytes 1544 | tf_op jit(solution)/shard_map/while/body/eval_jaxpr/ppermute | solution.py:14
  880.9 14.7 %collective-permute-start = (bf16[128,512]{1,0:T(8,128)(2,1)S(1)}, bf16[128,512]{1,0:T(8,128)(2,1)S(1)}, u32[]{:S(2)}, u32[]{:S(2)}) collective-permute-start(bf16[128,512]{1,0:T(8,128)(2,1)S(1)} %get-tuple-element.171), channel_id=1, source_target_pairs={{0,4},{4,8},{8,12},{12,16},{16,20},{20,24},{24,28},{28,32},{32,36}... | collective-permute-start | bytes 393224 | tf_op jit(solution)/shard_map/while/body/eval_jaxpr/ppermute | solution.py:14
  882.8 12.8 %collective-permute-start.1 = (s32[128]{0:T(128)S(1)}, s32[128]{0:T(128)S(1)}, u32[]{:S(2)}, u32[]{:S(2)}) collective-permute-start(s32[128]{0:T(128)S(1)} %get-tuple-element.172), channel_id=1, source_target_pairs={{0,4},{4,8},{8,12},{12,16},{16,20},{20,24},{24,28},{28,32},{32,36}... | collective-permute-start | bytes 1544 | tf_op jit(solution)/shard_map/while/body/eval_jaxpr/ppermute | solution.py:14
  895.7 13.8 %collective-permute-start = (bf16[128,512]{1,0:T(8,128)(2,1)S(1)}, bf16[128,512]{1,0:T(8,128)(2,1)S(1)}, u32[]{:S(2)}, u32[]{:S(2)}) collective-permute-start(bf16[128,512]{1,0:T(8,128)(2,1)S(1)} %get-tuple-element.171), channel_id=1, source_target_pairs={{0,4},{4,8},{8,12},{12,16},{16,20},{20,24},{24,28},{28,32},{32,36}... | collective-permute-start | bytes 393224 | tf_op jit(solution)/shard_map/while/body/eval_jaxpr/ppermute | solution.py:14
  897.6 11.8 %collective-permute-start.1 = (s32[128]{0:T(128)S(1)}, s32[128]{0:T(128)S(1)}, u32[]{:S(2)}, u32[]{:S(2)}) collective-permute-start(s32[128]{0:T(128)S(1)} %get-tuple-element.172), channel_id=1, source_target_pairs={{0,4},{4,8},{8,12},{12,16},{16,20},{20,24},{24,28},{28,32},{32,36}... | collective-permute-start | bytes 1544 | tf_op jit(solution)/shard_map/while/body/eval_jaxpr/ppermute | solution.py:14
  909.5 13.8 %collective-permute-start = (bf16[128,512]{1,0:T(8,128)(2,1)S(1)}, bf16[128,512]{1,0:T(8,128)(2,1)S(1)}, u32[]{:S(2)}, u32[]{:S(2)}) collective-permute-start(bf16[128,512]{1,0:T(8,128)(2,1)S(1)} %get-tuple-element.171), channel_id=1, source_target_pairs={{0,4},{4,8},{8,12},{12,16},{16,20},{20,24},{24,28},{28,32},{32,36}... | collective-permute-start | bytes 393224 | tf_op jit(solution)/shard_map/while/body/eval_jaxpr/ppermute | solution.py:14
  923.3 13.8 %collective-permute-start = (bf16[128,512]{1,0:T(8,128)(2,1)S(1)}, bf16[128,512]{1,0:T(8,128)(2,1)S(1)}, u32[]{:S(2)}, u32[]{:S(2)}) collective-permute-start(bf16[128,512]{1,0:T(8,128)(2,1)S(1)} %get-tuple-element.171), channel_id=1, source_target_pairs={{0,4},{4,8},{8,12},{12,16},{16,20},{20,24},{24,28},{28,32},{32,36}... | collective-permute-start | bytes 393224 | tf_op jit(solution)/shard_map/while/body/eval_jaxpr/ppermute | solution.py:14
  925.3 11.8 %collective-permute-start.1 = (s32[128]{0:T(128)S(1)}, s32[128]{0:T(128)S(1)}, u32[]{:S(2)}, u32[]{:S(2)}) collective-permute-start(s32[128]{0:T(128)S(1)} %get-tuple-element.172), channel_id=1, source_target_pairs={{0,4},{4,8},{8,12},{12,16},{16,20},{20,24},{24,28},{28,32},{32,36}... | collective-permute-start | bytes 1544 | tf_op jit(solution)/shard_map/while/body/eval_jaxpr/ppermute | solution.py:14
  937.2 13.8 %collective-permute-start = (bf16[128,512]{1,0:T(8,128)(2,1)S(1)}, bf16[128,512]{1,0:T(8,128)(2,1)S(1)}, u32[]{:S(2)}, u32[]{:S(2)}) collective-permute-start(bf16[128,512]{1,0:T(8,128)(2,1)S(1)} %get-tuple-element.171), channel_id=1, source_target_pairs={{0,4},{4,8},{8,12},{12,16},{16,20},{20,24},{24,28},{28,32},{32,36}... | collective-permute-start | bytes 393224 | tf_op jit(solution)/shard_map/while/body/eval_jaxpr/ppermute | solution.py:14
  951.0 13.8 %collective-permute-start = (bf16[128,512]{1,0:T(8,128)(2,1)S(1)}, bf16[128,512]{1,0:T(8,128)(2,1)S(1)}, u32[]{:S(2)}, u32[]{:S(2)}) collective-permute-start(bf16[128,512]{1,0:T(8,128)(2,1)S(1)} %get-tuple-element.171), channel_id=1, source_target_pairs={{0,4},{4,8},{8,12},{12,16},{16,20},{20,24},{24,28},{28,32},{32,36}... | collective-permute-start | bytes 393224 | tf_op jit(solution)/shard_map/while/body/eval_jaxpr/ppermute | solution.py:14
  952.9 11.8 %collective-permute-start.1 = (s32[128]{0:T(128)S(1)}, s32[128]{0:T(128)S(1)}, u32[]{:S(2)}, u32[]{:S(2)}) collective-permute-start(s32[128]{0:T(128)S(1)} %get-tuple-element.172), channel_id=1, source_target_pairs={{0,4},{4,8},{8,12},{12,16},{16,20},{20,24},{24,28},{28,32},{32,36}... | collective-permute-start | bytes 1544 | tf_op jit(solution)/shard_map/while/body/eval_jaxpr/ppermute | solution.py:14
  964.8 13.8 %collective-permute-start = (bf16[128,512]{1,0:T(8,128)(2,1)S(1)}, bf16[128,512]{1,0:T(8,128)(2,1)S(1)}, u32[]{:S(2)}, u32[]{:S(2)}) collective-permute-start(bf16[128,512]{1,0:T(8,128)(2,1)S(1)} %get-tuple-element.171), channel_id=1, source_target_pairs={{0,4},{4,8},{8,12},{12,16},{16,20},{20,24},{24,28},{28,32},{32,36}... | collective-permute-start | bytes 393224 | tf_op jit(solution)/shard_map/while/body/eval_jaxpr/ppermute | solution.py:14
  978.6 13.8 %collective-permute-start = (bf16[128,512]{1,0:T(8,128)(2,1)S(1)}, bf16[128,512]{1,0:T(8,128)(2,1)S(1)}, u32[]{:S(2)}, u32[]{:S(2)}) collective-permute-start(bf16[128,512]{1,0:T(8,128)(2,1)S(1)} %get-tuple-element.171), channel_id=1, source_target_pairs={{0,4},{4,8},{8,12},{12,16},{16,20},{20,24},{24,28},{28,32},{32,36}... | collective-permute-start | bytes 393224 | tf_op jit(solution)/shard_map/while/body/eval_jaxpr/ppermute | solution.py:14
  980.6 11.8 %collective-permute-start.1 = (s32[128]{0:T(128)S(1)}, s32[128]{0:T(128)S(1)}, u32[]{:S(2)}, u32[]{:S(2)}) collective-permute-start(s32[128]{0:T(128)S(1)} %get-tuple-element.172), channel_id=1, source_target_pairs={{0,4},{4,8},{8,12},{12,16},{16,20},{20,24},{24,28},{28,32},{32,36}... | collective-permute-start | bytes 1544 | tf_op jit(solution)/shard_map/while/body/eval_jaxpr/ppermute | solution.py:14
  992.5 13.8 %collective-permute-start = (bf16[128,512]{1,0:T(8,128)(2,1)S(1)}, bf16[128,512]{1,0:T(8,128)(2,1)S(1)}, u32[]{:S(2)}, u32[]{:S(2)}) collective-permute-start(bf16[128,512]{1,0:T(8,128)(2,1)S(1)} %get-tuple-element.171), channel_id=1, source_target_pairs={{0,4},{4,8},{8,12},{12,16},{16,20},{20,24},{24,28},{28,32},{32,36}... | collective-permute-start | bytes 393224 | tf_op jit(solution)/shard_map/while/body/eval_jaxpr/ppermute | solution.py:14
  (14 other events, 2502.9 us)
Sparse Core Ops, SparseCore 0:
  12.7 135.0 all-gather.7
  152.5 127.5 all-gather.9
  284.8 127.3 all-gather.11
  1015.8 31.6 reduce-scatter.3
